TPU v7x, 256 devices: a whole 4x4x8 slice. The times are simulated.
256 devices in a mesh: tm: 8 (over x_hi, y), azim: 32 (over z, x_lo, core).
Axes of the slice: x: 4 (x_hi: 2, x_lo: 2; x = x_hi * 2 + x_lo), y: 4, z: 8, core: 2. Of those that a mesh axis runs over, the one named last changes fastest.
Arguments:
- rotor_coeffs: float32 [64, 2, 32, 16384], P('tm', None, 'azim'), may hold values from -1.5 to 1.5
- mortar_weights: float32 [64, 2, 32, 16384], P('tm', None, 'azim'), may hold values from 0.2 to 1
- block_shifts: int32 [64], P('tm'), may hold values from 0 to 31
- stencil_offsets: int32 [64, 2], P('tm'), may hold values from -1 to 1
- reluctivity: float32 [32, 16384], P('azim'), may hold values from 0.5 to 2
- source: float32 [64, 2, 32, 16384], P('tm', None, 'azim'), may hold values from -3 to 3
Outputs:
- residual: float32 [64, 2, 32, 16384], P('tm', None, 'azim')
All inputs are finite; a program needn't handle non-finite values.
Results may differ from a plain program's by a relative error of at most 0.0001.
Values sent between devices are 32-bit elements; how exact they have to be, the bound alone decides.
A program may use at most 128 MiB of HBM per device.

v0:
```python
import itertools
import jax
import jax.numpy as jnp
import numpy as np
from jax import lax
from jax.sharding import PartitionSpec as P

KC = 64
NT = 64
LANES = 128


def shifted(value, axis, steps):
    count = lax.axis_size(axis)
    pairs = [(source, (source + steps) % count) for source in range(count)]
    return lax.ppermute(value, axis, pairs)


def harmonic_basis(sample_rows, coefficient_count):
    column = jnp.arange(coefficient_count, dtype=jnp.int32)
    harmonic_order = 2 * (column // 2) + 1
    phase_index = harmonic_order[None, :] * (2 * sample_rows[:, None] + 1) % (4 * NT)
    phase_angle = phase_index.astype(jnp.float32) * (jnp.pi / (2 * NT))
    return jnp.where(column[None, :] % 2 == 0, jnp.cos(phase_angle), jnp.sin(phase_angle))


def per_sample(flags, value):
    return flags.reshape((-1,) + (1,) * (value.ndim - 1))


def digit_table(stages, count):
    found = {}
    for bits in itertools.product((0, 1), repeat=len(stages)):
        found.setdefault(sum((b * s for b, s in zip(bits, stages))) % count, bits)
    return np.array([found[d] for d in range(count)], np.int32)


def barrel(value, amounts, stages, axis):
    count = lax.axis_size(axis)
    picks = jnp.take(jnp.asarray(digit_table(stages, count)), amounts % count, axis=0)
    for level, steps in enumerate(stages):
        moved = shifted(value, axis, steps)
        value = jnp.where(per_sample(picks[:, level] == 1, value), moved, value)
    return value


def body(rotor_coeffs, mortar_weights, block_shifts, stencil_offsets, reluctivity, source):
    local_c, comp, _, nodes = rotor_coeffs.shape
    local_j, sten = mortar_weights.shape[:2]
    rows = nodes // LANES
    parts = lax.axis_size("tm")
    chunk = rows // parts
    coeffs = lax.all_to_all(
        rotor_coeffs.reshape(local_c, comp, rows, LANES),
        "tm",
        split_axis=2,
        concat_axis=0,
        tiled=True,
    )
    weights = lax.all_to_all(
        mortar_weights.reshape(local_j, sten, rows, LANES),
        "tm",
        split_axis=2,
        concat_axis=0,
        tiled=True,
    )
    small = jnp.concatenate([block_shifts[:, None], stencil_offsets], axis=1).astype(jnp.float32)
    small = lax.all_gather(small, "tm", tiled=True).astype(jnp.int32)
    shifts, offsets = (small[:, 0], small[:, 1:])
    gain = lax.dynamic_slice_in_dim(
        reluctivity.reshape(rows, LANES), lax.axis_index("tm") * chunk, chunk, axis=0
    )
    table = harmonic_basis(jnp.arange(NT, dtype=jnp.int32), KC)
    samples = jnp.einsum("jc,capk->japk", table, coeffs, precision=lax.Precision.HIGHEST)
    orders = ((1, 2, 4, -8, 16), (16, 8, -4, 2, 1))
    fields = []
    for component in range(comp):
        turned = barrel(samples[:, component], shifts, orders[component % 2], "azim")
        from_left = shifted(turned, "azim", 1)
        from_right = shifted(turned, "azim", -1)
        field = jnp.zeros_like(turned)
        for stencil_entry in range(sten):
            offset = offsets[:, stencil_entry]
            neighbour = jnp.where(
                per_sample(offset == 0, turned),
                turned,
                jnp.where(per_sample(offset > 0, turned), from_right, from_left),
            )
            field = field + weights[:, stencil_entry] * neighbour
        fields.append(field)
    airgap_field = jnp.stack(fields, axis=1)
    square = jnp.sum(airgap_field * airgap_field, axis=1, keepdims=True)
    field_flux = gain[None, None] * (1.0 + square / (1.0 + square)) * airgap_field
    summed = jnp.einsum(
        "jc,japk->capk", table * (2.0 / NT), field_flux, precision=lax.Precision.HIGHEST
    )
    residual = lax.all_to_all(summed, "tm", split_axis=0, concat_axis=2, tiled=True)
    return residual.reshape(source.shape) - source


def solution(mesh):
    in_specs = (
        P("tm", None, "azim", None),
        P("tm", None, "azim", None),
        P("tm"),
        P("tm", None),
        P("azim", None),
        P("tm", None, "azim", None),
    )
    out_specs = P("tm", None, "azim", None)
    return jax.shard_map(body, mesh=mesh, in_specs=in_specs, out_specs=out_specs, check_vma=False)
```

profile of v0, /device:TPU:1, one launch (start us, length us, event | category | flops | bytes accessed | tf_op | source)
XLA Modules:
  0.0 249.5 jit_solution(8012935296902372771)
XLA Ops:
  0.0 3.0 %copy.42 = f32[8,2,128,128]{3,1,0,2:T(2,128)} copy(f32[8,2,128,128]{3,2,1,0:T(8,128)} %bitcast.73) | data formatting | bytes 2097152 | tf_op jit(solution)/shard_map/reshape | solution.py:54
  3.0 7.5 %all-to-all-start.1 = ((f32[8,2,128,128]{3,1,0,2:T(2,128)}), f32[8,2,128,128]{3,1,0,2:T(2,128)S(1)}, u32[]{:S(2)}, u32[]{:S(2)}) async-start(f32[8,2,128,128]{3,1,0,2:T(2,128)} %copy.42), calls=%async_computation.1 | async-start | bytes 2097152 | tf_op jit(solution)/shard_map/all_to_all | solution.py:53
  11.2 34.0 %all-gather = f32[8,8,3]{1,2,0:T(4,128)S(1)} all-gather(f32[1,8,3]{1,2,0:T(4,128)S(1)} %fusion.25), channel_id=1, replica_groups=mesh['tm'=8,'azim'=32] {'tm'}, dimensions={0}, use_global_device_ids=true | all-gather | bytes 864 | tf_op jit(solution)/shard_map/all_gather | solution.py:68
  47.6 5.6 %collective-permute-start = (f32[64,16,128]{2,0,1:T(8,128)S(1)}, f32[64,16,128]{2,0,1:T(8,128)S(1)}, u32[]{:S(2)}, u32[]{:S(2)}) collective-permute-start(f32[64,16,128]{2,0,1:T(8,128)S(1)} %get-tuple-element.22), channel_id=1, source_target_pairs={{0,1},{1,2},{2,3},{3,4},{4,5},{5,6},{6,7},{7,8},{8,9},{9,10},{10,1... | collective-permute-start | bytes 1572872 | tf_op jit(solution)/shard_map/ppermute | solution.py:16
  53.2 6.9 %collective-permute-start.7 = (f32[64,16,128]{2,0,1:T(8,128)S(1)}, f32[64,16,128]{2,0,1:T(8,128)S(1)}, u32[]{:S(2)}, u32[]{:S(2)}) collective-permute-start(f32[64,16,128]{2,0,1:T(8,128)S(1)} %get-tuple-element.23), channel_id=1, source_target_pairs={{0,16},{1,17},{2,18},{3,19},{4,20},{5,21},{6,22},{7,23},{8,24},{9,... | collective-permute-start | bytes 1572872 | tf_op jit(solution)/shard_map/ppermute | solution.py:16
  62.0 12.7 %collective-permute-done.7 = f32[64,16,128]{2,0,1:T(8,128)S(1)} collective-permute-done((f32[64,16,128]{2,0,1:T(8,128)S(1)}, f32[64,16,128]{2,0,1:T(8,128)S(1)}, u32[]{:S(2)}, u32[]{:S(2)}) %collective-permute-start.7) | collective-permute-done | bytes 524320 | tf_op jit(solution)/shard_map/ppermute | solution.py:16
  74.9 7.1 %collective-permute-start.1 = (f32[64,16,128]{2,0,1:T(8,128)S(1)}, f32[64,16,128]{2,0,1:T(8,128)S(1)}, u32[]{:S(2)}, u32[]{:S(2)}) collective-permute-start(f32[64,16,128]{2,0,1:T(8,128)S(1)} %get-tuple-element.20), channel_id=1, source_target_pairs={{0,2},{1,3},{2,4},{3,5},{4,6},{5,7},{6,8},{7,9},{8,10},{9,11},{10,... | collective-permute-start | bytes 1572872 | tf_op jit(solution)/shard_map/ppermute | solution.py:16
  82.0 9.7 %collective-permute-start.8 = (f32[64,16,128]{2,0,1:T(8,128)S(1)}, f32[64,16,128]{2,0,1:T(8,128)S(1)}, u32[]{:S(2)}, u32[]{:S(2)}) collective-permute-start(f32[64,16,128]{2,0,1:T(8,128)S(1)} %get-tuple-element.21), channel_id=1, source_target_pairs={{0,8},{1,9},{2,10},{3,11},{4,12},{5,13},{6,14},{7,15},{8,16},{9,17... | collective-permute-start | bytes 1572872 | tf_op jit(solution)/shard_map/ppermute | solution.py:16
  91.7 8.9 %collective-permute-done.1 = f32[64,16,128]{2,0,1:T(8,128)S(1)} collective-permute-done((f32[64,16,128]{2,0,1:T(8,128)S(1)}, f32[64,16,128]{2,0,1:T(8,128)S(1)}, u32[]{:S(2)}, u32[]{:S(2)}) %collective-permute-start.1) | collective-permute-done | bytes 524320 | tf_op jit(solution)/shard_map/ppermute | solution.py:16
  101.8 11.3 %collective-permute-done.8 = f32[64,16,128]{2,0,1:T(8,128)S(1)} collective-permute-done((f32[64,16,128]{2,0,1:T(8,128)S(1)}, f32[64,16,128]{2,0,1:T(8,128)S(1)}, u32[]{:S(2)}, u32[]{:S(2)}) %collective-permute-start.8) | collective-permute-done | bytes 524320 | tf_op jit(solution)/shard_map/ppermute | solution.py:16
  113.3 11.0 %collective-permute-done.2 = f32[64,16,128]{2,0,1:T(8,128)S(1)} collective-permute-done((f32[64,16,128]{2,0,1:T(8,128)S(1)}, f32[64,16,128]{2,0,1:T(8,128)S(1)}, u32[]{:S(2)}, u32[]{:S(2)}) %collective-permute-start.2) | collective-permute-done | bytes 524320 | tf_op jit(solution)/shard_map/ppermute | solution.py:16
  126.5 10.6 %collective-permute-start.10 = (f32[64,16,128]{2,0,1:T(8,128)S(1)}, f32[64,16,128]{2,0,1:T(8,128)S(1)}, u32[]{:S(2)}, u32[]{:S(2)}) collective-permute-start(f32[64,16,128]{2,0,1:T(8,128)S(1)} %broadcast_select_fusion.2), channel_id=1, source_target_pairs={{0,2},{1,3},{2,4},{3,5},{4,6},{5,7},{6,8},{7,9},{8,10},{9,11},{10,... | collective-permute-start | bytes 1572872 | tf_op jit(solution)/shard_map/ppermute | solution.py:16
  137.1 12.8 %collective-permute-done.3 = f32[64,16,128]{2,0,1:T(8,128)S(1)} collective-permute-done((f32[64,16,128]{2,0,1:T(8,128)S(1)}, f32[64,16,128]{2,0,1:T(8,128)S(1)}, u32[]{:S(2)}, u32[]{:S(2)}) %collective-permute-start.3) | collective-permute-done | bytes 524320 | tf_op jit(solution)/shard_map/ppermute | solution.py:16
  150.0 2.1 collective-permute-start.4
  152.3 26.2 %collective-permute-start.11 = (f32[64,16,128]{2,0,1:T(8,128)S(1)}, f32[64,16,128]{2,0,1:T(8,128)}, u32[]{:S(2)}, u32[]{:S(2)}) collective-permute-start(f32[64,16,128]{2,0,1:T(8,128)S(1)} %broadcast_select_fusion.3), channel_id=1, source_target_pairs={{0,1},{1,2},{2,3},{3,4},{4,5},{5,6},{6,7},{7,8},{8,9},{9,10},{10,1... | collective-permute-start | bytes 1572872 | tf_op jit(solution)/shard_map/ppermute | solution.py:16
  178.5 1.8 copy.37
  180.3 3.6 %all-to-all-start = ((f32[8,2,128,128]{3,1,0,2:T(2,128)}), f32[8,2,128,128]{3,1,0,2:T(2,128)S(1)}, u32[]{:S(2)}, u32[]{:S(2)}) async-start(f32[8,2,128,128]{3,1,0,2:T(2,128)} %copy.37), calls=%async_computation | async-start | bytes 2097152 | tf_op jit(solution)/shard_map/all_to_all | solution.py:60
  185.7 7.0 %collective-permute-start.6 = (f32[64,16,128]{2,0,1:T(8,128)S(1)}, f32[64,16,128]{2,0,1:T(8,128)}, u32[]{:S(2)}, u32[]{:S(2)}) collective-permute-start(f32[64,16,128]{2,0,1:T(8,128)S(1)} %broadcast_select_fusion.9), channel_id=1, source_target_pairs={{0,1},{1,2},{2,3},{3,4},{4,5},{5,6},{6,7},{7,8},{8,9},{9,10},{10,1... | collective-permute-start | bytes 1572872 | tf_op jit(solution)/shard_map/ppermute | solution.py:16
  195.1 5.5 %collective-permute-start.12 = (f32[64,16,128]{2,0,1:T(8,128)S(1)}, f32[64,16,128]{2,0,1:T(8,128)S(1)}, u32[]{:S(2)}, u32[]{:S(2)}) collective-permute-start(f32[64,16,128]{2,0,1:T(8,128)S(1)} %broadcast_select_fusion.4), channel_id=1, source_target_pairs={{0,31},{1,0},{2,1},{3,2},{4,3},{5,4},{6,5},{7,6},{8,7},{9,8},{10,9... | collective-permute-start | bytes 1572872 | tf_op jit(solution)/shard_map/ppermute | solution.py:16
  200.6 5.0 %all-to-all-done = f32[8,2,128,128]{3,1,0,2:T(2,128)S(1)} async-done(((f32[8,2,128,128]{3,1,0,2:T(2,128)}), f32[8,2,128,128]{3,1,0,2:T(2,128)S(1)}, u32[]{:S(2)}, u32[]{:S(2)}) %all-to-all-start) | async-done | bytes 1048608 | tf_op jit(solution)/shard_map/all_to_all | solution.py:60
  206.6 9.3 %collective-permute-done.5 = f32[64,16,128]{2,0,1:T(8,128)S(1)} collective-permute-done((f32[64,16,128]{2,0,1:T(8,128)S(1)}, f32[64,16,128]{2,0,1:T(8,128)S(1)}, u32[]{:S(2)}, u32[]{:S(2)}) %collective-permute-start.5) | collective-permute-done | bytes 524320 | tf_op jit(solution)/shard_map/ppermute | solution.py:16
  215.9 10.1 %collective-permute-done.12 = f32[64,16,128]{2,0,1:T(8,128)S(1)} collective-permute-done((f32[64,16,128]{2,0,1:T(8,128)S(1)}, f32[64,16,128]{2,0,1:T(8,128)S(1)}, u32[]{:S(2)}, u32[]{:S(2)}) %collective-permute-start.12) | collective-permute-done | bytes 524320 | tf_op jit(solution)/shard_map/ppermute | solution.py:16
  229.8 16.5 %all_to_all.51 = f32[64,2,16,128]{3,2,1,0:T(8,128)S(1)} all-to-all(f32[64,2,16,128]{3,2,1,0:T(8,128)S(1)} %copy.46), channel_id=1, replica_groups=mesh['tm'=8,'azim'=32] {'tm'}, dimensions={0} | all-to-all | bytes 2097152 | tf_op jit(solution)/shard_map/all_to_all | solution.py:97
  247.5 2.1 sub.12
  (60 shorter events, 19.0 us)
Async XLA Ops:
  0.0 200.6 %copy-start = (f32[1,16384]{1,0:T(1,128)S(1)}, f32[1,16384]{1,0:T(1,128)}, u32[]{:S(2)}) copy-start(f32[1,16384]{1,0:T(1,128)} %param.14) | copy-start | bytes 196612
  3.0 42.3 %all-to-all-start.1 = ((f32[8,2,128,128]{3,1,0,2:T(2,128)}), f32[8,2,128,128]{3,1,0,2:T(2,128)S(1)}, u32[]{:S(2)}, u32[]{:S(2)}) async-start(f32[8,2,128,128]{3,1,0,2:T(2,128)} %copy.42), calls=%async_computation.1 | async-start | bytes 2097152 | tf_op jit(solution)/shard_map/all_to_all | solution.py:53
  10.5 0.7 copy-start.5
  10.5 0.7 copy-start.6
  47.5 12.7 %copy-start.1 = (s32[32,5]{1,0:T(8,128)S(1)}, s32[32,5]{1,0:T(8,128)}, u32[]{:S(2)}) copy-start(s32[32,5]{1,0:T(8,128)} %constant.99.clone2.1) | copy-start | bytes 1924
  47.6 14.4 %collective-permute-start = (f32[64,16,128]{2,0,1:T(8,128)S(1)}, f32[64,16,128]{2,0,1:T(8,128)S(1)}, u32[]{:S(2)}, u32[]{:S(2)}) collective-permute-start(f32[64,16,128]{2,0,1:T(8,128)S(1)} %get-tuple-element.22), channel_id=1, source_target_pairs={{0,1},{1,2},{2,3},{3,4},{4,5},{5,6},{6,7},{7,8},{8,9},{9,10},{10,1... | collective-permute-start | bytes 1572872 | tf_op jit(solution)/shard_map/ppermute | solution.py:16
  53.2 21.5 %collective-permute-start.7 = (f32[64,16,128]{2,0,1:T(8,128)S(1)}, f32[64,16,128]{2,0,1:T(8,128)S(1)}, u32[]{:S(2)}, u32[]{:S(2)}) collective-permute-start(f32[64,16,128]{2,0,1:T(8,128)S(1)} %get-tuple-element.23), channel_id=1, source_target_pairs={{0,16},{1,17},{2,18},{3,19},{4,20},{5,21},{6,22},{7,23},{8,24},{9,... | collective-permute-start | bytes 1572872 | tf_op jit(solution)/shard_map/ppermute | solution.py:16
  60.2 0.7 copy-start.2
  74.9 25.7 %collective-permute-start.1 = (f32[64,16,128]{2,0,1:T(8,128)S(1)}, f32[64,16,128]{2,0,1:T(8,128)S(1)}, u32[]{:S(2)}, u32[]{:S(2)}) collective-permute-start(f32[64,16,128]{2,0,1:T(8,128)S(1)} %get-tuple-element.20), channel_id=1, source_target_pairs={{0,2},{1,3},{2,4},{3,5},{4,6},{5,7},{6,8},{7,9},{8,10},{9,11},{10,... | collective-permute-start | bytes 1572872 | tf_op jit(solution)/shard_map/ppermute | solution.py:16
  82.0 31.1 %collective-permute-start.8 = (f32[64,16,128]{2,0,1:T(8,128)S(1)}, f32[64,16,128]{2,0,1:T(8,128)S(1)}, u32[]{:S(2)}, u32[]{:S(2)}) collective-permute-start(f32[64,16,128]{2,0,1:T(8,128)S(1)} %get-tuple-element.21), channel_id=1, source_target_pairs={{0,8},{1,9},{2,10},{3,11},{4,12},{5,13},{6,14},{7,15},{8,16},{9,17... | collective-permute-start | bytes 1572872 | tf_op jit(solution)/shard_map/ppermute | solution.py:16
  100.7 23.6 %collective-permute-start.2 = (f32[64,16,128]{2,0,1:T(8,128)S(1)}, f32[64,16,128]{2,0,1:T(8,128)S(1)}, u32[]{:S(2)}, u32[]{:S(2)}) collective-permute-start(f32[64,16,128]{2,0,1:T(8,128)S(1)} %broadcast_select_fusion.6), channel_id=1, source_target_pairs={{0,4},{1,5},{2,6},{3,7},{4,8},{5,9},{6,10},{7,11},{8,12},{9,13},{1... | collective-permute-start | bytes 1572872 | tf_op jit(solution)/shard_map/ppermute | solution.py:16
  113.2 13.1 %collective-permute-start.9 = (f32[64,16,128]{2,0,1:T(8,128)S(1)}, f32[64,16,128]{2,0,1:T(8,128)S(1)}, u32[]{:S(2)}, u32[]{:S(2)}) collective-permute-start(f32[64,16,128]{2,0,1:T(8,128)S(1)} %broadcast_select_fusion.1), channel_id=1, source_target_pairs={{0,28},{1,29},{2,30},{3,31},{4,0},{5,1},{6,2},{7,3},{8,4},{9,5},{1... | collective-permute-start | bytes 1572872 | tf_op jit(solution)/shard_map/ppermute | solution.py:16
  124.4 25.5 %collective-permute-start.3 = (f32[64,16,128]{2,0,1:T(8,128)S(1)}, f32[64,16,128]{2,0,1:T(8,128)S(1)}, u32[]{:S(2)}, u32[]{:S(2)}) collective-permute-start(f32[64,16,128]{2,0,1:T(8,128)S(1)} %broadcast_select_fusion.7), channel_id=1, source_target_pairs={{0,24},{1,25},{2,26},{3,27},{4,28},{5,29},{6,30},{7,31},{8,0},{9,1... | collective-permute-start | bytes 1572872 | tf_op jit(solution)/shard_map/ppermute | solution.py:16
  126.5 25.6 %collective-permute-start.10 = (f32[64,16,128]{2,0,1:T(8,128)S(1)}, f32[64,16,128]{2,0,1:T(8,128)S(1)}, u32[]{:S(2)}, u32[]{:S(2)}) collective-permute-start(f32[64,16,128]{2,0,1:T(8,128)S(1)} %broadcast_select_fusion.2), channel_id=1, source_target_pairs={{0,2},{1,3},{2,4},{3,5},{4,6},{5,7},{6,8},{7,9},{8,10},{9,11},{10,... | collective-permute-start | bytes 1572872 | tf_op jit(solution)/shard_map/ppermute | solution.py:16
  150.0 28.5 %copy-start.4 = (f32[8,2,1,16384]{3,2,1,0:T(1,128)S(1)}, f32[8,2,1,16384]{3,2,1,0:T(1,128)}, u32[]{:S(2)}) copy-start(f32[8,2,1,16384]{3,2,1,0:T(1,128)} %param.11) | copy-start | bytes 3145732
  150.0 33.8 %collective-permute-start.4 = (f32[64,16,128]{2,0,1:T(8,128)S(1)}, f32[64,16,128]{2,0,1:T(8,128)S(1)}, u32[]{:S(2)}, u32[]{:S(2)}) collective-permute-start(f32[64,16,128]{2,0,1:T(8,128)S(1)} %broadcast_select_fusion.8), channel_id=1, source_target_pairs={{0,16},{1,17},{2,18},{3,19},{4,20},{5,21},{6,22},{7,23},{8,24},{9,... | collective-permute-start | bytes 1572872 | tf_op jit(solution)/shard_map/ppermute | solution.py:16
  152.3 41.7 %collective-permute-start.11 = (f32[64,16,128]{2,0,1:T(8,128)S(1)}, f32[64,16,128]{2,0,1:T(8,128)}, u32[]{:S(2)}, u32[]{:S(2)}) collective-permute-start(f32[64,16,128]{2,0,1:T(8,128)S(1)} %broadcast_select_fusion.3), channel_id=1, source_target_pairs={{0,1},{1,2},{2,3},{3,4},{4,5},{5,6},{6,7},{7,8},{8,9},{9,10},{10,1... | collective-permute-start | bytes 1572872 | tf_op jit(solution)/shard_map/ppermute | solution.py:16
  180.3 25.4 %all-to-all-start = ((f32[8,2,128,128]{3,1,0,2:T(2,128)}), f32[8,2,128,128]{3,1,0,2:T(2,128)S(1)}, u32[]{:S(2)}, u32[]{:S(2)}) async-start(f32[8,2,128,128]{3,1,0,2:T(2,128)} %copy.37), calls=%async_computation | async-start | bytes 2097152 | tf_op jit(solution)/shard_map/all_to_all | solution.py:60
  184.0 31.9 %collective-permute-start.5 = (f32[64,16,128]{2,0,1:T(8,128)S(1)}, f32[64,16,128]{2,0,1:T(8,128)S(1)}, u32[]{:S(2)}, u32[]{:S(2)}) collective-permute-start(f32[64,16,128]{2,0,1:T(8,128)S(1)} %broadcast_select_fusion.9), channel_id=1, source_target_pairs={{0,31},{1,0},{2,1},{3,2},{4,3},{5,4},{6,5},{7,6},{8,7},{9,8},{10,9... | collective-permute-start | bytes 1572872 | tf_op jit(solution)/shard_map/ppermute | solution.py:16
  185.7 30.2 %collective-permute-start.6 = (f32[64,16,128]{2,0,1:T(8,128)S(1)}, f32[64,16,128]{2,0,1:T(8,128)}, u32[]{:S(2)}, u32[]{:S(2)}) collective-permute-start(f32[64,16,128]{2,0,1:T(8,128)S(1)} %broadcast_select_fusion.9), channel_id=1, source_target_pairs={{0,1},{1,2},{2,3},{3,4},{4,5},{5,6},{6,7},{7,8},{8,9},{9,10},{10,1... | collective-permute-start | bytes 1572872 | tf_op jit(solution)/shard_map/ppermute | solution.py:16
  195.1 30.9 %collective-permute-start.12 = (f32[64,16,128]{2,0,1:T(8,128)S(1)}, f32[64,16,128]{2,0,1:T(8,128)S(1)}, u32[]{:S(2)}, u32[]{:S(2)}) collective-permute-start(f32[64,16,128]{2,0,1:T(8,128)S(1)} %broadcast_select_fusion.4), channel_id=1, source_target_pairs={{0,31},{1,0},{2,1},{3,2},{4,3},{5,4},{6,5},{7,6},{8,7},{9,8},{10,9... | collective-permute-start | bytes 1572872 | tf_op jit(solution)/shard_map/ppermute | solution.py:16
  200.6 25.4 %collective-permute-start.13 = (f32[64,16,128]{2,0,1:T(8,128)S(1)}, f32[64,16,128]{2,0,1:T(8,128)}, u32[]{:S(2)}, u32[]{:S(2)}) collective-permute-start(f32[64,16,128]{2,0,1:T(8,128)S(1)} %broadcast_select_fusion.4), channel_id=1, source_target_pairs={{0,1},{1,2},{2,3},{3,4},{4,5},{5,6},{6,7},{7,8},{8,9},{9,10},{10,1... | collective-permute-start | bytes 1572872 | tf_op jit(solution)/shard_map/ppermute | solution.py:16
  246.2 1.2 copy-start.3
where the time goes:
time: 250 us
  starting transfers between devices  95.6 us (38%)
  waiting for transfers between devices  83.4 us (33%)
  blocking collectives  50.5 us (20%)
  local copies, waits for them, and re-layouts  10.1 us (4%)
  other arithmetic  6.77 us (3%)
  matrix products  2.96 us (1%)
    ppermute x14, starting transfers between devices, shifted(): return lax.ppermute(value, axis, pairs)  84.5 us
    ppermute x14, waiting for transfers between devices, shifted(): return lax.ppermute(value, axis, pairs)  78.3 us
    all_gather x1, blocking collectives, body(): small = lax.all_gather(small, 'tm', tiled=True).astype(jnp.int32)  34 us
    all_to_all x1, blocking collectives, body(): lax.all_to_all(summed, 'tm', split_axis=0, concat_axis=2, tiled=True)  16.5 us
    all_to_all x1, starting transfers between devices, body(): lax.all_to_all(rotor_coeffs.reshape(local_c, comp, rows, LANES), 'tm', sp...  7.48 us
    all_to_all x1, waiting for transfers between devices, body(): lax.all_to_all(mortar_weights.reshape(local_j, sten, rows, LANES), 'tm',...  5.02 us
  transfers between devices with their start and end apart: 16, of which 10 were waited for; matrix products, arithmetic and copies ran while one was open for 3% of the time, Pallas kernels for 0%

commit v1 on v0

--- a/solution.py
+++ b/solution.py
@@ -50,13 +50,12 @@
     rows = nodes // LANES
     parts = lax.axis_size("tm")
     chunk = rows // parts
-    coeffs = lax.all_to_all(
-        rotor_coeffs.reshape(local_c, comp, rows, LANES),
-        "tm",
-        split_axis=2,
-        concat_axis=0,
-        tiled=True,
-    )
+    payload = rotor_coeffs.reshape(local_c, comp, rows, LANES)
+    low = lax.axis_size("tm")
+    res = jnp.split(payload, low, axis=2)
+    row_out = jnp.stack(res)
+    q_next = lax.all_to_all(row_out, split_axis=0, concat_axis=0, axis_name="tm")
+    coeffs = jnp.concatenate(q_next, axis=0)
     weights = lax.all_to_all(
         mortar_weights.reshape(local_j, sten, rows, LANES),
         "tm",

time: 250 us -> 249 us (level)
    reshape x1 -> x0, local copies, waits for them, and re-layouts: 3.04 us -> none  [body(): rotor_coeffs.reshape(local_c, comp, rows, LANES)]
where the time goes in v1:
time: 249 us; the launch traced here: 248 us
  starting transfers between devices  95.1 us (38%)
  waiting for transfers between devices  83.8 us (34%)
  blocking collectives  50.4 us (20%)
  local copies, waits for them, and re-layouts  9.53 us (4%)
  other arithmetic  6.77 us (3%)
    ppermute x14, starting transfers between devices, shifted(): return lax.ppermute(value, axis, pairs)  84.1 us
    ppermute x14, waiting for transfers between devices, shifted(): return lax.ppermute(value, axis, pairs)  78.5 us
    all_gather x1, blocking collectives, body(): small = lax.all_gather(small, 'tm', tiled=True).astype(jnp.int32)  34 us
    all_to_all x1, blocking collectives, body(): lax.all_to_all(summed, 'tm', split_axis=0, concat_axis=2, tiled=True)  16.4 us
    all_to_all x1, starting transfers between devices, body(): lax.all_to_all(row_out, split_axis=0, concat_axis=0, axis_name='tm')  7.48 us
    all_to_all x1, waiting for transfers between devices, body(): lax.all_to_all(mortar_weights.reshape(local_j, sten, rows, LANES), 'tm',...  5.38 us
  transfers between devices with their start and end apart: 16, of which 10 were waited for; matrix products, arithmetic and copies ran while one was open for 3% of the time, Pallas kernels for 0%

profile of v1, /device:TPU:1, one launch (start us, length us, event | category | flops | bytes accessed | tf_op | source)
XLA Modules:
  0.0 248.4 jit_solution(12084259370579526650)
XLA Ops:
  2.9 7.5 %all-to-all-start.1 = ((f32[8,8,2,16,128]{4,1,3,2,0:T(8,128)}), f32[8,8,2,16,128]{4,1,3,2,0:T(8,128)S(1)}, u32[]{:S(2)}, u32[]{:S(2)}) async-start(f32[8,8,2,16,128]{4,1,3,2,0:T(8,128)} %copy.55), calls=%async_computation.1 | async-start | bytes 2097152 | tf_op jit(solution)/shard_map/all_to_all | solution.py:57
  11.0 34.0 %all-gather = f32[8,8,3]{1,2,0:T(4,128)S(1)} all-gather(f32[1,8,3]{1,2,0:T(4,128)S(1)} %fusion.33), channel_id=1, replica_groups=mesh['tm'=8,'azim'=32] {'tm'}, dimensions={0}, use_global_device_ids=true | all-gather | bytes 864 | tf_op jit(solution)/shard_map/all_gather | solution.py:67
  46.5 5.6 %collective-permute-start = (f32[64,16,128]{2,0,1:T(8,128)S(1)}, f32[64,16,128]{2,0,1:T(8,128)S(1)}, u32[]{:S(2)}, u32[]{:S(2)}) collective-permute-start(f32[64,16,128]{2,0,1:T(8,128)S(1)} %get-tuple-element.22), channel_id=1, source_target_pairs={{0,1},{1,2},{2,3},{3,4},{4,5},{5,6},{6,7},{7,8},{8,9},{9,10},{10,1... | collective-permute-start | bytes 1572872 | tf_op jit(solution)/shard_map/ppermute | solution.py:16
  52.2 6.9 %collective-permute-start.7 = (f32[64,16,128]{2,0,1:T(8,128)S(1)}, f32[64,16,128]{2,0,1:T(8,128)S(1)}, u32[]{:S(2)}, u32[]{:S(2)}) collective-permute-start(f32[64,16,128]{2,0,1:T(8,128)S(1)} %get-tuple-element.23), channel_id=1, source_target_pairs={{0,16},{1,17},{2,18},{3,19},{4,20},{5,21},{6,22},{7,23},{8,24},{9,... | collective-permute-start | bytes 1572872 | tf_op jit(solution)/shard_map/ppermute | solution.py:16
  60.9 12.7 %collective-permute-done.7 = f32[64,16,128]{2,0,1:T(8,128)S(1)} collective-permute-done((f32[64,16,128]{2,0,1:T(8,128)S(1)}, f32[64,16,128]{2,0,1:T(8,128)S(1)}, u32[]{:S(2)}, u32[]{:S(2)}) %collective-permute-start.7) | collective-permute-done | bytes 524320 | tf_op jit(solution)/shard_map/ppermute | solution.py:16
  73.8 7.1 %collective-permute-start.1 = (f32[64,16,128]{2,0,1:T(8,128)S(1)}, f32[64,16,128]{2,0,1:T(8,128)S(1)}, u32[]{:S(2)}, u32[]{:S(2)}) collective-permute-start(f32[64,16,128]{2,0,1:T(8,128)S(1)} %get-tuple-element.20), channel_id=1, source_target_pairs={{0,2},{1,3},{2,4},{3,5},{4,6},{5,7},{6,8},{7,9},{8,10},{9,11},{10,... | collective-permute-start | bytes 1572872 | tf_op jit(solution)/shard_map/ppermute | solution.py:16
  81.0 9.7 %collective-permute-start.8 = (f32[64,16,128]{2,0,1:T(8,128)S(1)}, f32[64,16,128]{2,0,1:T(8,128)S(1)}, u32[]{:S(2)}, u32[]{:S(2)}) collective-permute-start(f32[64,16,128]{2,0,1:T(8,128)S(1)} %get-tuple-element.21), channel_id=1, source_target_pairs={{0,8},{1,9},{2,10},{3,11},{4,12},{5,13},{6,14},{7,15},{8,16},{9,17... | collective-permute-start | bytes 1572872 | tf_op jit(solution)/shard_map/ppermute | solution.py:16
  90.6 8.9 %collective-permute-done.1 = f32[64,16,128]{2,0,1:T(8,128)S(1)} collective-permute-done((f32[64,16,128]{2,0,1:T(8,128)S(1)}, f32[64,16,128]{2,0,1:T(8,128)S(1)}, u32[]{:S(2)}, u32[]{:S(2)}) %collective-permute-start.1) | collective-permute-done | bytes 524320 | tf_op jit(solution)/shard_map/ppermute | solution.py:16
  100.7 11.3 %collective-permute-done.8 = f32[64,16,128]{2,0,1:T(8,128)S(1)} collective-permute-done((f32[64,16,128]{2,0,1:T(8,128)S(1)}, f32[64,16,128]{2,0,1:T(8,128)S(1)}, u32[]{:S(2)}, u32[]{:S(2)}) %collective-permute-start.8) | collective-permute-done | bytes 524320 | tf_op jit(solution)/shard_map/ppermute | solution.py:16
  112.3 11.0 %collective-permute-done.2 = f32[64,16,128]{2,0,1:T(8,128)S(1)} collective-permute-done((f32[64,16,128]{2,0,1:T(8,128)S(1)}, f32[64,16,128]{2,0,1:T(8,128)S(1)}, u32[]{:S(2)}, u32[]{:S(2)}) %collective-permute-start.2) | collective-permute-done | bytes 524320 | tf_op jit(solution)/shard_map/ppermute | solution.py:16
  125.5 10.6 %collective-permute-start.10 = (f32[64,16,128]{2,0,1:T(8,128)S(1)}, f32[64,16,128]{2,0,1:T(8,128)S(1)}, u32[]{:S(2)}, u32[]{:S(2)}) collective-permute-start(f32[64,16,128]{2,0,1:T(8,128)S(1)} %broadcast_select_fusion.2), channel_id=1, source_target_pairs={{0,2},{1,3},{2,4},{3,5},{4,6},{5,7},{6,8},{7,9},{8,10},{9,11},{10,... | collective-permute-start | bytes 1572872 | tf_op jit(solution)/shard_map/ppermute | solution.py:16
  136.0 12.8 %collective-permute-done.3 = f32[64,16,128]{2,0,1:T(8,128)S(1)} collective-permute-done((f32[64,16,128]{2,0,1:T(8,128)S(1)}, f32[64,16,128]{2,0,1:T(8,128)S(1)}, u32[]{:S(2)}, u32[]{:S(2)}) %collective-permute-start.3) | collective-permute-done | bytes 524320 | tf_op jit(solution)/shard_map/ppermute | solution.py:16
  149.0 2.1 collective-permute-start.4
  151.2 26.0 %collective-permute-start.11 = (f32[64,16,128]{2,0,1:T(8,128)S(1)}, f32[64,16,128]{2,0,1:T(8,128)}, u32[]{:S(2)}, u32[]{:S(2)}) collective-permute-start(f32[64,16,128]{2,0,1:T(8,128)S(1)} %broadcast_select_fusion.3), channel_id=1, source_target_pairs={{0,1},{1,2},{2,3},{3,4},{4,5},{5,6},{6,7},{7,8},{8,9},{9,10},{10,1... | collective-permute-start | bytes 1572872 | tf_op jit(solution)/shard_map/ppermute | solution.py:16
  177.2 1.8 copy.50
  179.0 3.6 %all-to-all-start = ((f32[8,2,128,128]{3,1,0,2:T(2,128)}), f32[8,2,128,128]{3,1,0,2:T(2,128)S(1)}, u32[]{:S(2)}, u32[]{:S(2)}) async-start(f32[8,2,128,128]{3,1,0,2:T(2,128)} %copy.50), calls=%async_computation | async-start | bytes 2097152 | tf_op jit(solution)/shard_map/all_to_all | solution.py:59
  182.7 2.1 collective-permute-start.5
  184.8 7.0 %collective-permute-start.6 = (f32[64,16,128]{2,0,1:T(8,128)S(1)}, f32[64,16,128]{2,0,1:T(8,128)}, u32[]{:S(2)}, u32[]{:S(2)}) collective-permute-start(f32[64,16,128]{2,0,1:T(8,128)S(1)} %broadcast_select_fusion.9), channel_id=1, source_target_pairs={{0,1},{1,2},{2,3},{3,4},{4,5},{5,6},{6,7},{7,8},{8,9},{9,10},{10,1... | collective-permute-start | bytes 1572872 | tf_op jit(solution)/shard_map/ppermute | solution.py:16
  194.5 4.9 %collective-permute-start.12 = (f32[64,16,128]{2,0,1:T(8,128)S(1)}, f32[64,16,128]{2,0,1:T(8,128)S(1)}, u32[]{:S(2)}, u32[]{:S(2)}) collective-permute-start(f32[64,16,128]{2,0,1:T(8,128)S(1)} %broadcast_select_fusion.4), channel_id=1, source_target_pairs={{0,31},{1,0},{2,1},{3,2},{4,3},{5,4},{6,5},{7,6},{8,7},{9,8},{10,9... | collective-permute-start | bytes 1572872 | tf_op jit(solution)/shard_map/ppermute | solution.py:16
  199.4 5.4 %all-to-all-done = f32[8,2,128,128]{3,1,0,2:T(2,128)S(1)} async-done(((f32[8,2,128,128]{3,1,0,2:T(2,128)}), f32[8,2,128,128]{3,1,0,2:T(2,128)S(1)}, u32[]{:S(2)}, u32[]{:S(2)}) %all-to-all-start) | async-done | bytes 1048608 | tf_op jit(solution)/shard_map/all_to_all | solution.py:59
  205.7 9.2 %collective-permute-done.5 = f32[64,16,128]{2,0,1:T(8,128)S(1)} collective-permute-done((f32[64,16,128]{2,0,1:T(8,128)S(1)}, f32[64,16,128]{2,0,1:T(8,128)S(1)}, u32[]{:S(2)}, u32[]{:S(2)}) %collective-permute-start.5) | collective-permute-done | bytes 524320 | tf_op jit(solution)/shard_map/ppermute | solution.py:16
  214.9 10.0 %collective-permute-done.12 = f32[64,16,128]{2,0,1:T(8,128)S(1)} collective-permute-done((f32[64,16,128]{2,0,1:T(8,128)S(1)}, f32[64,16,128]{2,0,1:T(8,128)S(1)}, u32[]{:S(2)}, u32[]{:S(2)}) %collective-permute-start.12) | collective-permute-done | bytes 524320 | tf_op jit(solution)/shard_map/ppermute | solution.py:16
  228.7 16.4 %all_to_all.38 = f32[64,2,16,128]{3,2,1,0:T(8,128)S(1)} all-to-all(f32[64,2,16,128]{3,2,1,0:T(8,128)S(1)} %copy.58), channel_id=1, replica_groups=mesh['tm'=8,'azim'=32] {'tm'}, dimensions={0} | all-to-all | bytes 2097152 | tf_op jit(solution)/shard_map/all_to_all | solution.py:96
  246.3 2.1 sub.12
  (68 shorter events, 19.5 us)
Async XLA Ops:
  0.0 199.4 %copy-start = (f32[1,16384]{1,0:T(1,128)S(1)}, f32[1,16384]{1,0:T(1,128)}, u32[]{:S(2)}) copy-start(f32[1,16384]{1,0:T(1,128)} %param.14) | copy-start | bytes 196612
  2.9 42.3 %all-to-all-start.1 = ((f32[8,8,2,16,128]{4,1,3,2,0:T(8,128)}), f32[8,8,2,16,128]{4,1,3,2,0:T(8,128)S(1)}, u32[]{:S(2)}, u32[]{:S(2)}) async-start(f32[8,8,2,16,128]{4,1,3,2,0:T(8,128)} %copy.55), calls=%async_computation.1 | async-start | bytes 2097152 | tf_op jit(solution)/shard_map/all_to_all | solution.py:57
  10.3 0.7 copy-start.5
  10.3 0.7 copy-start.6
  46.4 12.7 %copy-start.1 = (s32[32,5]{1,0:T(8,128)S(1)}, s32[32,5]{1,0:T(8,128)}, u32[]{:S(2)}) copy-start(s32[32,5]{1,0:T(8,128)} %constant.99.clone2.1) | copy-start | bytes 1924
  46.5 14.4 %collective-permute-start = (f32[64,16,128]{2,0,1:T(8,128)S(1)}, f32[64,16,128]{2,0,1:T(8,128)S(1)}, u32[]{:S(2)}, u32[]{:S(2)}) collective-permute-start(f32[64,16,128]{2,0,1:T(8,128)S(1)} %get-tuple-element.22), channel_id=1, source_target_pairs={{0,1},{1,2},{2,3},{3,4},{4,5},{5,6},{6,7},{7,8},{8,9},{9,10},{10,1... | collective-permute-start | bytes 1572872 | tf_op jit(solution)/shard_map/ppermute | solution.py:16
  52.2 21.5 %collective-permute-start.7 = (f32[64,16,128]{2,0,1:T(8,128)S(1)}, f32[64,16,128]{2,0,1:T(8,128)S(1)}, u32[]{:S(2)}, u32[]{:S(2)}) collective-permute-start(f32[64,16,128]{2,0,1:T(8,128)S(1)} %get-tuple-element.23), channel_id=1, source_target_pairs={{0,16},{1,17},{2,18},{3,19},{4,20},{5,21},{6,22},{7,23},{8,24},{9,... | collective-permute-start | bytes 1572872 | tf_op jit(solution)/shard_map/ppermute | solution.py:16
  59.1 0.7 copy-start.2
  73.8 25.7 %collective-permute-start.1 = (f32[64,16,128]{2,0,1:T(8,128)S(1)}, f32[64,16,128]{2,0,1:T(8,128)S(1)}, u32[]{:S(2)}, u32[]{:S(2)}) collective-permute-start(f32[64,16,128]{2,0,1:T(8,128)S(1)} %get-tuple-element.20), channel_id=1, source_target_pairs={{0,2},{1,3},{2,4},{3,5},{4,6},{5,7},{6,8},{7,9},{8,10},{9,11},{10,... | collective-permute-start | bytes 1572872 | tf_op jit(solution)/shard_map/ppermute | solution.py:16
  81.0 31.1 %collective-permute-start.8 = (f32[64,16,128]{2,0,1:T(8,128)S(1)}, f32[64,16,128]{2,0,1:T(8,128)S(1)}, u32[]{:S(2)}, u32[]{:S(2)}) collective-permute-start(f32[64,16,128]{2,0,1:T(8,128)S(1)} %get-tuple-element.21), channel_id=1, source_target_pairs={{0,8},{1,9},{2,10},{3,11},{4,12},{5,13},{6,14},{7,15},{8,16},{9,17... | collective-permute-start | bytes 1572872 | tf_op jit(solution)/shard_map/ppermute | solution.py:16
  99.7 23.6 %collective-permute-start.2 = (f32[64,16,128]{2,0,1:T(8,128)S(1)}, f32[64,16,128]{2,0,1:T(8,128)S(1)}, u32[]{:S(2)}, u32[]{:S(2)}) collective-permute-start(f32[64,16,128]{2,0,1:T(8,128)S(1)} %broadcast_select_fusion.6), channel_id=1, source_target_pairs={{0,4},{1,5},{2,6},{3,7},{4,8},{5,9},{6,10},{7,11},{8,12},{9,13},{1... | collective-permute-start | bytes 1572872 | tf_op jit(solution)/shard_map/ppermute | solution.py:16
  112.2 13.1 %collective-permute-start.9 = (f32[64,16,128]{2,0,1:T(8,128)S(1)}, f32[64,16,128]{2,0,1:T(8,128)S(1)}, u32[]{:S(2)}, u32[]{:S(2)}) collective-permute-start(f32[64,16,128]{2,0,1:T(8,128)S(1)} %broadcast_select_fusion.1), channel_id=1, source_target_pairs={{0,28},{1,29},{2,30},{3,31},{4,0},{5,1},{6,2},{7,3},{8,4},{9,5},{1... | collective-permute-start | bytes 1572872 | tf_op jit(solution)/shard_map/ppermute | solution.py:16
  123.4 25.5 %collective-permute-start.3 = (f32[64,16,128]{2,0,1:T(8,128)S(1)}, f32[64,16,128]{2,0,1:T(8,128)S(1)}, u32[]{:S(2)}, u32[]{:S(2)}) collective-permute-start(f32[64,16,128]{2,0,1:T(8,128)S(1)} %broadcast_select_fusion.7), channel_id=1, source_target_pairs={{0,24},{1,25},{2,26},{3,27},{4,28},{5,29},{6,30},{7,31},{8,0},{9,1... | collective-permute-start | bytes 1572872 | tf_op jit(solution)/shard_map/ppermute | solution.py:16
  125.5 25.6 %collective-permute-start.10 = (f32[64,16,128]{2,0,1:T(8,128)S(1)}, f32[64,16,128]{2,0,1:T(8,128)S(1)}, u32[]{:S(2)}, u32[]{:S(2)}) collective-permute-start(f32[64,16,128]{2,0,1:T(8,128)S(1)} %broadcast_select_fusion.2), channel_id=1, source_target_pairs={{0,2},{1,3},{2,4},{3,5},{4,6},{5,7},{6,8},{7,9},{8,10},{9,11},{10,... | collective-permute-start | bytes 1572872 | tf_op jit(solution)/shard_map/ppermute | solution.py:16
  149.0 28.2 %copy-start.4 = (f32[8,2,1,16384]{3,2,1,0:T(1,128)S(1)}, f32[8,2,1,16384]{3,2,1,0:T(1,128)}, u32[]{:S(2)}) copy-start(f32[8,2,1,16384]{3,2,1,0:T(1,128)} %param.11) | copy-start | bytes 3145732
  149.0 33.6 %collective-permute-start.4 = (f32[64,16,128]{2,0,1:T(8,128)S(1)}, f32[64,16,128]{2,0,1:T(8,128)S(1)}, u32[]{:S(2)}, u32[]{:S(2)}) collective-permute-start(f32[64,16,128]{2,0,1:T(8,128)S(1)} %broadcast_select_fusion.8), channel_id=1, source_target_pairs={{0,16},{1,17},{2,18},{3,19},{4,20},{5,21},{6,22},{7,23},{8,24},{9,... | collective-permute-start | bytes 1572872 | tf_op jit(solution)/shard_map/ppermute | solution.py:16
  151.2 42.1 %collective-permute-start.11 = (f32[64,16,128]{2,0,1:T(8,128)S(1)}, f32[64,16,128]{2,0,1:T(8,128)}, u32[]{:S(2)}, u32[]{:S(2)}) collective-permute-start(f32[64,16,128]{2,0,1:T(8,128)S(1)} %broadcast_select_fusion.3), channel_id=1, source_target_pairs={{0,1},{1,2},{2,3},{3,4},{4,5},{5,6},{6,7},{7,8},{8,9},{9,10},{10,1... | collective-permute-start | bytes 1572872 | tf_op jit(solution)/shard_map/ppermute | solution.py:16
  179.0 25.8 %all-to-all-start = ((f32[8,2,128,128]{3,1,0,2:T(2,128)}), f32[8,2,128,128]{3,1,0,2:T(2,128)S(1)}, u32[]{:S(2)}, u32[]{:S(2)}) async-start(f32[8,2,128,128]{3,1,0,2:T(2,128)} %copy.50), calls=%async_computation | async-start | bytes 2097152 | tf_op jit(solution)/shard_map/all_to_all | solution.py:59
  182.7 32.2 %collective-permute-start.5 = (f32[64,16,128]{2,0,1:T(8,128)S(1)}, f32[64,16,128]{2,0,1:T(8,128)S(1)}, u32[]{:S(2)}, u32[]{:S(2)}) collective-permute-start(f32[64,16,128]{2,0,1:T(8,128)S(1)} %broadcast_select_fusion.9), channel_id=1, source_target_pairs={{0,31},{1,0},{2,1},{3,2},{4,3},{5,4},{6,5},{7,6},{8,7},{9,8},{10,9... | collective-permute-start | bytes 1572872 | tf_op jit(solution)/shard_map/ppermute | solution.py:16
  184.8 30.1 %collective-permute-start.6 = (f32[64,16,128]{2,0,1:T(8,128)S(1)}, f32[64,16,128]{2,0,1:T(8,128)}, u32[]{:S(2)}, u32[]{:S(2)}) collective-permute-start(f32[64,16,128]{2,0,1:T(8,128)S(1)} %broadcast_select_fusion.9), channel_id=1, source_target_pairs={{0,1},{1,2},{2,3},{3,4},{4,5},{5,6},{6,7},{7,8},{8,9},{9,10},{10,1... | collective-permute-start | bytes 1572872 | tf_op jit(solution)/shard_map/ppermute | solution.py:16
  194.5 30.4 %collective-permute-start.12 = (f32[64,16,128]{2,0,1:T(8,128)S(1)}, f32[64,16,128]{2,0,1:T(8,128)S(1)}, u32[]{:S(2)}, u32[]{:S(2)}) collective-permute-start(f32[64,16,128]{2,0,1:T(8,128)S(1)} %broadcast_select_fusion.4), channel_id=1, source_target_pairs={{0,31},{1,0},{2,1},{3,2},{4,3},{5,4},{6,5},{7,6},{8,7},{9,8},{10,9... | collective-permute-start | bytes 1572872 | tf_op jit(solution)/shard_map/ppermute | solution.py:16
  199.4 25.6 %collective-permute-start.13 = (f32[64,16,128]{2,0,1:T(8,128)S(1)}, f32[64,16,128]{2,0,1:T(8,128)}, u32[]{:S(2)}, u32[]{:S(2)}) collective-permute-start(f32[64,16,128]{2,0,1:T(8,128)S(1)} %broadcast_select_fusion.4), channel_id=1, source_target_pairs={{0,1},{1,2},{2,3},{3,4},{4,5},{5,6},{6,7},{7,8},{8,9},{9,10},{10,1... | collective-permute-start | bytes 1572872 | tf_op jit(solution)/shard_map/ppermute | solution.py:16
  245.1 1.2 copy-start.3
